TPU v7x, 128 devices: a whole 4x4x4 slice. The times are simulated.
128 devices in a mesh: row: 8 (over y, core), col: 16 (over x, z).
Axes of the slice: x: 4, y: 4, z: 4, core: 2. Of those that a mesh axis runs over, the one named last changes fastest.
Arguments:
- strip_columns: float32 [4096, 32, 256], P(('row', 'col')), may hold values from -0.0048828125 to 0.0048828125
- tile_columns: float32 [4096, 4, 32, 256], P(('row', 'col')), may hold values from -6 to 6
- barrier_weights: float32 [4096, 32], P(('row', 'col')), may hold values from 0.01 to 100
- column_counts: int32 [4096], P(('row', 'col')), may hold values from 1 to 32
- tile_lists: int32 [4096, 4], P(('row', 'col')), may hold values from 0 to 127, all different within a row; in each aligned block of 32 rows (0 to 31, 32 to 63, ...) at most 2 rows name the same one
Outputs:
- panel_factor: float32 [256, 256], replicated
- strip_update: float32 [256, 32768], P(None, ('row', 'col'))
Inputs may be any that keep to these rules, and one draw needn't show every extreme that they name: `tile_lists`: each block lists 4 different column tiles; among the 32 blocks of one device no tile is listed more than 2 times, and in some device one tile is listed exactly 2 times.
All inputs are finite; a program needn't handle non-finite values.
Results may differ from a plain program's by a relative error of at most 0.0001.
Values sent between devices are 32-bit elements; how exact they have to be, the bound alone decides.
A program may use at most 192 MiB of HBM per device.

v0:
```python
import jax
import jax.numpy as jnp
from jax import lax
from jax.sharding import PartitionSpec as P


def per_device(strip_columns, tile_columns, barrier_weights, column_counts, tile_lists):
    highest = lax.Precision.HIGHEST
    blocks, block_width, strip_rows = strip_columns.shape
    touched = tile_columns.shape[1]
    own_width = tile_columns.shape[3]
    devices = lax.axis_size(("row", "col"))
    live_mask = jnp.arange(block_width, dtype=jnp.int32)[None, :] < column_counts[:, None]
    live_weight = jnp.where(live_mask, barrier_weights, 0.0)
    scaled = strip_columns * live_weight[:, :, None]
    local_diagonal = lax.dot_general(
        scaled, strip_columns, (((0, 1), (0, 1)), ((), ())), precision=highest
    )
    diagonal_block = lax.psum(local_diagonal, ("row", "col"))
    item_count = blocks * touched
    capacity = max(2, 2 * item_count // devices)
    targets = tile_lists.reshape(item_count)
    one_hot = (targets[:, None] == jnp.arange(devices, dtype=jnp.int32)[None, :]).astype(jnp.int32)
    earlier = jnp.cumsum(one_hot, axis=0) - one_hot
    ranked = jnp.sum(earlier * one_hot, axis=1)
    slot_index = targets * capacity + ranked
    slot_item = (
        jnp.full((devices * capacity,), -1, jnp.int32)
        .at[slot_index]
        .set(jnp.arange(item_count, dtype=jnp.int32))
    )
    filled = slot_item >= 0
    picked = jnp.maximum(slot_item, 0)
    send_strip = scaled[picked // touched]
    send_tile = tile_columns.reshape(item_count, block_width, own_width)[picked]
    outgoing = jnp.where(
        filled[:, None, None], jnp.concatenate([send_strip, send_tile], axis=2), 0.0
    )
    incoming = lax.all_to_all(outgoing, ("row", "col"), split_axis=0, concat_axis=0, tiled=True)
    tile_sum = lax.dot_general(
        incoming[:, :, :strip_rows],
        incoming[:, :, strip_rows:],
        (((0, 1), (0, 1)), ((), ())),
        precision=highest,
    )
    panel_factor = jnp.linalg.cholesky(diagonal_block)
    strip_update = jax.scipy.linalg.solve_triangular(panel_factor, tile_sum, lower=True)
    return (panel_factor, strip_update)


def solution(mesh):
    return jax.shard_map(
        per_device,
        mesh=mesh,
        in_specs=(
            P(("row", "col"), None, None),
            P(("row", "col"), None, None, None),
            P(("row", "col"), None),
            P(("row", "col")),
            P(("row", "col"), None),
        ),
        out_specs=(P(), P(None, ("row", "col"))),
        check_vma=False,
    )
```

profile of v0, /device:TPU:1, one launch (start us, length us, event | category | flops | bytes accessed | tf_op | source)
XLA Modules:
  0.0 456.5 jit_solution(12866232470006165996)
XLA Ops:
  7.2 0.7 broadcast_multiply_fusion.2
  7.8 0.8 copy.22
  8.6 0.1 copy.21
  8.7 0.1 mul.31
  8.8 0.1 eq.15
  8.9 0.1 fusion.17
  9.0 0.2 reduce_window_sum.11
  9.2 0.2 select_reduce_fusion
  9.4 1.0 scatter_custom_fusion
  10.4 0.8 fusion.18
  11.2 0.0 copy-start
  11.2 6.6 %gather_fusion.1 = f32[256,32,256]{2,1,0:T(8,128)} fusion(f32[128,32,256]{2,1,0:T(8,128)} %bitcast.43, s32[1024]{0:T(1024)S(1)} %get-tuple-element.34), kind=kCustom, calls=%fused_computation.1 | custom fusion | bytes 16778240 | tf_op jit(solution)/shard_map/gather | solution.py:35
  17.8 0.0 copy-done
  17.8 0.2 broadcast_multiply_fusion
  18.0 4.3 gather_fusion
  22.3 11.6 %maximum_select_fusion = f32[256,32,512]{2,1,0:T(8,128)} fusion(f32[256,32,256]{2,1,0:T(8,128)} %gather_fusion.1, f32[256,32,256]{2,1,0:T(8,128)} %gather_fusion, pred[256]{0:T(512)(128)(4,1)S(1)} %broadcast_compare_fusion), kind=kLoop, calls=%fused_computation.5 | loop fusion | flops 8388608 | bytes 33554688 | tf_op jit(solution)/shard_map/jit(_where)/select_n | solution.py:36
  34.0 12.0 %all-to-all-start = ((f32[256,32,512]{2,1,0:T(8,128)}), f32[256,32,512]{2,1,0:T(8,128)}, u32[]{:S(2)}, u32[]{:S(2)}) async-start(f32[256,32,512]{2,1,0:T(8,128)} %maximum_select_fusion), calls=%async_computation | async-start | bytes 33554432 | tf_op jit(solution)/shard_map/all_to_all | solution.py:39
  46.0 0.4 all-reduce.3.cloned.1.call-start
  46.4 2.7 convolution_bitcast_fusion
  49.1 0.0 all-reduce.3.cloned.1.call-update
  49.1 297.1 %all-reduce.3.cloned.1.call-done = f32[256,256]{0,1:T(8,128)} async-done(((f32[256,256]{0,1:T(8,128)}), f32[256,256]{0,1:T(8,128)}) %all-reduce.3.cloned.1.call-update) | async-done | bytes 262160 | tf_op jit(solution)/shard_map/psum | solution.py:19
  346.2 1.1 copy.20
  347.3 1.0 fusion.8
  348.3 11.7 %cholesky.51 = f32[128,128]{1,0:T(8,128)S(1)} custom-call(f32[128,128]{1,0:T(8,128)S(1)} %cholesky.121), custom_call_target="Cholesky" | custom-call | tf_op jit(solution)/shard_map/jit(cholesky)/cholesky | solution.py:46
  360.1 9.8 %custom-call.15 = f32[1,128,128]{1,2,0:T(8,128)S(1)} custom-call(f32[1,128,128]{2,1,0:T(8,128)S(1)} %get-tuple-element.27), custom_call_target="InvertDiagBlocksLowerTriangular" | custom-call | tf_op jit(solution)/shard_map/jit(cholesky)/cholesky | solution.py:46
  369.9 0.2 constant_dynamic-update-slice_fusion.1
  370.1 0.3 convolution_subtract_fusion.1
  370.4 22.5 %cholesky.107 = f32[128,128]{1,0:T(8,128)S(1)} custom-call(f32[128,128]{1,0:T(8,128)S(1)} %convolution_subtract_fusion.1), custom_call_target="Cholesky" | custom-call | tf_op jit(solution)/shard_map/jit(cholesky)/cholesky | solution.py:46
  392.9 0.6 compare_reduce_fusion
  394.9 0.7 fusion.9
  395.6 0.1 triangular_solve.44
  395.7 4.0 while.1
  395.7 0.6 fusion.30
  396.3 1.4 bitcast_dynamic-update-slice_fusion.2
  397.7 0.6 fusion.30
  398.3 1.4 bitcast_dynamic-update-slice_fusion.2
  399.7 19.7 %custom-call.16 = f32[2,128,128]{1,2,0:T(8,128)S(1)} custom-call(f32[2,128,128]{2,1,0:T(8,128)S(1)} %get-tuple-element.9), custom_call_target="InvertDiagBlocksLowerTriangular" | custom-call | tf_op jit(solution)/shard_map/jit(_solve_triangular)/triangular_solve | solution.py:47
  419.4 0.0 all-to-all-done
  419.4 6.8 %fusion.23 = (f32[256,32,256]{2,1,0:T(8,128)S(1)}, f32[256,32,256]{2,1,0:T(8,128)S(1)}) fusion(f32[256,32,512]{2,1,0:T(8,128)} %all-to-all-done), kind=kLoop, calls=%fused_computation.57 | loop fusion | bytes 33554432 | tf_op jit(solution)/shard_map/slice | solution.py:41
  426.2 21.6 %fusion.3 = f32[256,256]{1,0:T(8,128)S(1)} fusion(f32[256,32,256]{2,1,0:T(8,128)S(1)} %get-tuple-element.23, f32[256,32,256]{2,1,0:T(8,128)S(1)} %get-tuple-element.22), kind=kOutput, calls=%fused_computation.9 | convolution fusion | flops 6442450944 | bytes 17039360 | tf_op jit(solution)/shard_map/dot_general | solution.py:40
  447.8 0.3 fusion.10
  448.1 0.3 convolution_subtract_fusion
  448.4 0.3 fusion.13
  448.7 0.7 pad_maximum_fusion
  (13 shorter events, 0.1 us)
Async XLA Ops:
  11.2 6.6 %copy-start = (f32[32,32,256]{2,1,0:T(8,128)S(1)}, f32[32,32,256]{2,1,0:T(8,128)}, u32[]{:S(2)}) copy-start(f32[32,32,256]{2,1,0:T(8,128)} %param.5) | copy-start | bytes 3145732
  34.0 385.4 %all-to-all-start = ((f32[256,32,512]{2,1,0:T(8,128)}), f32[256,32,512]{2,1,0:T(8,128)}, u32[]{:S(2)}, u32[]{:S(2)}) async-start(f32[256,32,512]{2,1,0:T(8,128)} %maximum_select_fusion), calls=%async_computation | async-start | bytes 33554432 | tf_op jit(solution)/shard_map/all_to_all | solution.py:39
  46.0 300.3 %all-reduce.3.cloned.1.call-start = ((), (), s32[]{:S(2)}) async-start(), calls=%async_computation.1 | async-start | bytes 524288 | tf_op jit(solution)/shard_map/psum | solution.py:19
Sparse Core Ops, SparseCore 0:
  52.1 294.0 all-reduce.2
where the time goes:
time: 460 us; the launch traced here: 456 us
  waiting for transfers between devices  297 us (65%)
  other arithmetic  80.6 us (18%)
  matrix products  25.6 us (6%)
  local copies, waits for them, and re-layouts  24.9 us (5%)
  between operations  15.8 us (3%)
  starting transfers between devices  12.4 us (3%)
    psum x1, waiting for transfers between devices, per_device(): diagonal_block = lax.psum(local_diagonal, ('row', 'col'))  297 us
    another operation x6, other arithmetic, per_device(): panel_factor = jnp.linalg.cholesky(diagonal_block)  44.7 us
    dot_general x1, matrix products, per_device(): lax.dot_general(incoming[:, :, :strip_rows], incoming[:, :, strip_rows:],...  21.6 us
    another operation x4, other arithmetic, per_device(): jax.scipy.linalg.solve_triangular(panel_factor, tile_sum, lower=True)  21.1 us
    all_to_all x1, starting transfers between devices, per_device(): lax.all_to_all(outgoing, ('row', 'col'), split_axis=0, concat_axis=0, til...  12 us
    select_n x1, other arithmetic, per_device(): jnp.where(filled[:, None, None], jnp.concatenate([send_strip, send_tile],...  11.6 us
  transfers between devices with their start and end apart: 2, of which 1 were waited for; matrix products, arithmetic and copies ran while one was open for 16% of the time, Pallas kernels for 0%

commit v1 on v0

--- a/solution.py
+++ b/solution.py
@@ -16,7 +16,7 @@
     local_diagonal = lax.dot_general(
         scaled, strip_columns, (((0, 1), (0, 1)), ((), ())), precision=highest
     )
-    diagonal_block = lax.psum(local_diagonal, ("row", "col"))
+    diagonal_block = jnp.sum(lax.all_gather(local_diagonal, ("row", "col")), axis=0)
     item_count = blocks * touched
     capacity = max(2, 2 * item_count // devices)
     targets = tile_lists.reshape(item_count)

time: 460 us -> 442 us (0.961); the launches traced: 456 us -> 433 us
  waiting for transfers between devices: 297 us -> 273 us
    psum x1 -> x0, waiting for transfers between devices: 297 us -> none  [per_device(): diagonal_block = lax.psum(local_diagonal, ('row', 'col'))]
    all_to_all x1, waiting for transfers between devices: 0.01 us -> 273 us  [per_device(): lax.all_to_all(outgoing, ('row', 'col'), split_axis=0, concat_axis=0, til...]
    reduce_sum x0 -> x1, other arithmetic: none -> 12.2 us  [per_device(): jnp.sum(lax.all_gather(local_diagonal, ('row', 'col')), axis=0)]
    another operation x6, other arithmetic: 44.7 us -> 33.9 us  [per_device(): panel_factor = jnp.linalg.cholesky(diagonal_block)]
  transfers between devices with their start and end apart: 2 -> 2, of which waited for: 1 -> 1; matrix products, arithmetic and copies ran while one was open for 16% -> 13% of each run, Pallas kernels for 0% -> 0%
where the time goes in v1:
time: 442 us; the launch traced here: 433 us
  waiting for transfers between devices  273 us (62%)
  other arithmetic  81.4 us (18%)
  matrix products  27.2 us (6%)
  local copies, waits for them, and re-layouts  24.5 us (6%)
  between operations  15.8 us (4%)
  starting transfers between devices  12 us (3%)
    all_to_all x1, waiting for transfers between devices, per_device(): lax.all_to_all(outgoing, ('row', 'col'), split_axis=0, concat_axis=0, til...  273 us
    another operation x6, other arithmetic, per_device(): panel_factor = jnp.linalg.cholesky(diagonal_block)  33.9 us
    dot_general x1, matrix products, per_device(): lax.dot_general(incoming[:, :, :strip_rows], incoming[:, :, strip_rows:],...  21.6 us
    another operation x4, other arithmetic, per_device(): jax.scipy.linalg.solve_triangular(panel_factor, tile_sum, lower=True)  21.4 us
    reduce_sum x1, other arithmetic, per_device(): jnp.sum(lax.all_gather(local_diagonal, ('row', 'col')), axis=0)  12.2 us
    all_to_all x1, starting transfers between devices, per_device(): lax.all_to_all(outgoing, ('row', 'col'), split_axis=0, concat_axis=0, til...  12 us
    select_n x1, other arithmetic, per_device(): jnp.where(filled[:, None, None], jnp.concatenate([send_strip, send_tile],...  11.7 us
  transfers between devices with their start and end apart: 2, of which 1 were waited for; matrix products, arithmetic and copies ran while one was open for 13% of the time, Pallas kernels for 0%

profile of v1, /device:TPU:1, one launch (start us, length us, event | category | flops | bytes accessed | tf_op | source)
XLA Modules:
  0.0 433.5 jit_solution(64877964339892035)
XLA Ops:
  7.2 0.0 all-gather.3.cloned.1.call-start
  7.2 0.8 fusion.18
  8.0 4.2 convolution_bitcast_fusion
  12.2 0.0 all-gather.3.cloned.1.call-update
  12.3 0.8 copy.19
  13.0 0.7 broadcast_multiply_fusion.2
  13.7 0.1 copy.18
  13.8 0.1 mul.31
  13.9 0.1 eq.15
  14.0 0.1 fusion.17
  14.1 0.2 reduce_window_sum.11
  14.3 0.2 select_reduce_fusion
  14.5 1.0 scatter_custom_fusion
  15.5 0.0 copy-start
  15.5 6.6 %gather_fusion.1 = f32[256,32,256]{2,1,0:T(8,128)} fusion(f32[128,32,256]{2,1,0:T(8,128)} %bitcast.45, s32[1024]{0:T(1024)S(1)} %get-tuple-element.34), kind=kCustom, calls=%fused_computation.1 | custom fusion | bytes 16778240 | tf_op jit(solution)/shard_map/gather | solution.py:35
  22.1 0.0 copy-done
  22.1 0.2 broadcast_multiply_fusion
  22.3 4.3 gather_fusion
  26.6 11.7 %maximum_select_fusion = f32[256,32,512]{2,1,0:T(8,128)} fusion(f32[256,32,256]{2,1,0:T(8,128)} %gather_fusion.1, f32[256,32,256]{2,1,0:T(8,128)} %gather_fusion, pred[256]{0:T(512)(128)(4,1)S(1)} %broadcast_compare_fusion), kind=kLoop, calls=%fused_computation.5 | loop fusion | flops 8388608 | bytes 33554688 | tf_op jit(solution)/shard_map/jit(_where)/select_n | solution.py:36
  38.4 12.0 %all-to-all-start = ((f32[256,32,512]{2,1,0:T(8,128)}), f32[256,32,512]{2,1,0:T(8,128)}, u32[]{:S(2)}, u32[]{:S(2)}) async-start(f32[256,32,512]{2,1,0:T(8,128)} %maximum_select_fusion), calls=%async_computation | async-start | bytes 33554432 | tf_op jit(solution)/shard_map/all_to_all | solution.py:39
  50.4 272.5 %all-to-all-done = f32[256,32,512]{2,1,0:T(8,128)} async-done(((f32[256,32,512]{2,1,0:T(8,128)}), f32[256,32,512]{2,1,0:T(8,128)}, u32[]{:S(2)}, u32[]{:S(2)}) %all-to-all-start) | async-done | bytes 16777248 | tf_op jit(solution)/shard_map/all_to_all | solution.py:39
  322.9 7.3 %fusion.23 = (f32[256,32,256]{2,1,0:T(8,128)S(1)}, f32[256,32,256]{2,1,0:T(8,128)S(1)}) fusion(f32[256,32,512]{2,1,0:T(8,128)} %all-to-all-done), kind=kLoop, calls=%fused_computation.57 | loop fusion | bytes 33554432 | tf_op jit(solution)/shard_map/slice | solution.py:41
  330.2 21.6 %fusion.3 = f32[256,256]{1,0:T(8,128)S(1)} fusion(f32[256,32,256]{2,1,0:T(8,128)S(1)} %get-tuple-element.23, f32[256,32,256]{2,1,0:T(8,128)S(1)} %get-tuple-element.22), kind=kOutput, calls=%fused_computation.9 | convolution fusion | flops 6442450944 | bytes 17039360 | tf_op jit(solution)/shard_map/dot_general | solution.py:40
  351.7 0.0 all-gather.3.cloned.1.call-done
  351.8 12.2 %reduce_sum.20 = f32[256,256]{1,0:T(8,128)S(1)} reduce(f32[128,256,256]{2,1,0:T(8,128)} %bitcast.44, f32[]{:T(128)} %constant.101.clone.1), dimensions={0}, to_apply=%region_0.1 | reduce | flops 8323072 | bytes 33816580 | tf_op jit(solution)/shard_map/reduce_sum | solution.py:19
  364.0 0.1 copy.17
  364.2 11.7 %cholesky.51 = f32[128,128]{1,0:T(8,128)S(1)} custom-call(f32[128,128]{1,0:T(8,128)S(1)} %cholesky.121), custom_call_target="Cholesky" | custom-call | tf_op jit(solution)/shard_map/jit(cholesky)/cholesky | solution.py:46
  375.9 9.8 %custom-call.15 = f32[1,128,128]{1,2,0:T(8,128)S(1)} custom-call(f32[1,128,128]{2,1,0:T(8,128)S(1)} %get-tuple-element.27), custom_call_target="InvertDiagBlocksLowerTriangular" | custom-call | tf_op jit(solution)/shard_map/jit(cholesky)/cholesky | solution.py:46
  385.7 0.2 constant_dynamic-update-slice_fusion.1
  386.0 0.3 convolution_subtract_fusion.1
  386.2 11.7 %cholesky.107 = f32[128,128]{1,0:T(8,128)S(1)} custom-call(f32[128,128]{1,0:T(8,128)S(1)} %convolution_subtract_fusion.1), custom_call_target="Cholesky" | custom-call | tf_op jit(solution)/shard_map/jit(cholesky)/cholesky | solution.py:46
  398.0 0.6 compare_reduce_fusion
  399.9 0.7 fusion.9
  400.7 0.1 triangular_solve.44
  400.7 4.1 while.1
  400.7 0.6 fusion.30
  401.3 1.4 bitcast_dynamic-update-slice_fusion.2
  402.8 0.6 fusion.30
  403.4 1.4 bitcast_dynamic-update-slice_fusion.2
  404.8 19.9 %custom-call.16 = f32[2,128,128]{1,2,0:T(8,128)S(1)} custom-call(f32[2,128,128]{2,1,0:T(8,128)S(1)} %get-tuple-element.9), custom_call_target="InvertDiagBlocksLowerTriangular" | custom-call | tf_op jit(solution)/shard_map/jit(_solve_triangular)/triangular_solve | solution.py:47
  424.8 0.3 fusion.10
  425.1 0.3 convolution_subtract_fusion
  425.3 0.3 fusion.13
  425.7 0.7 pad_maximum_fusion
  (14 shorter events, 0.2 us)
Async XLA Ops:
  7.2 344.6 %all-gather.3.cloned.1.call-start = ((), (), s32[]{:S(2)}) async-start(), calls=%async_computation.1 | async-start | bytes 33816576 | tf_op jit(solution)/shard_map/all_gather | solution.py:19
  15.5 6.6 %copy-start = (f32[32,32,256]{2,1,0:T(8,128)S(1)}, f32[32,32,256]{2,1,0:T(8,128)}, u32[]{:S(2)}) copy-start(f32[32,32,256]{2,1,0:T(8,128)} %param.5) | copy-start | bytes 3145732
  38.4 284.5 %all-to-all-start = ((f32[256,32,512]{2,1,0:T(8,128)}), f32[256,32,512]{2,1,0:T(8,128)}, u32[]{:S(2)}, u32[]{:S(2)}) async-start(f32[256,32,512]{2,1,0:T(8,128)} %maximum_select_fusion), calls=%async_computation | async-start | bytes 33554432 | tf_op jit(solution)/shard_map/all_to_all | solution.py:39
Sparse Core Ops, SparseCore 0:
  12.4 302.9 all-gather.2

commit v2 on v0

--- a/solution.py
+++ b/solution.py
@@ -16,7 +16,7 @@
     local_diagonal = lax.dot_general(
         scaled, strip_columns, (((0, 1), (0, 1)), ((), ())), precision=highest
     )
-    diagonal_block = lax.psum(local_diagonal, ("row", "col"))
+    diagonal_block = lax.psum(lax.psum(local_diagonal, "row"), "col")
     item_count = blocks * touched
     capacity = max(2, 2 * item_count // devices)
     targets = tile_lists.reshape(item_count)

time: 460 us -> 451 us (0.980)
  other arithmetic: 80.6 us -> 69.9 us
    another operation x6, other arithmetic: 44.7 us -> 33.9 us  [per_device(): panel_factor = jnp.linalg.cholesky(diagonal_block)]
    psum x1 -> x2, waiting for transfers between devices: 297 us -> 297 us  [per_device(): diagonal_block = lax.psum(lax.psum(local_diagonal, 'row'), 'col')]
  transfers between devices with their start and end apart: 2 -> 3, of which waited for: 1 -> 2; matrix products, arithmetic and copies ran while one was open for 16% -> 14% of each run, Pallas kernels for 0% -> 0%
where the time goes in v2:
time: 451 us; the launch traced here: 446 us
  waiting for transfers between devices  297 us (66%)
  other arithmetic  69.9 us (15%)
  matrix products  25.7 us (6%)
  local copies, waits for them, and re-layouts  25.1 us (6%)
  between operations  15.8 us (4%)
  starting transfers between devices  12.5 us (3%)
    psum x2, waiting for transfers between devices, per_device(): diagonal_block = lax.psum(lax.psum(local_diagonal, 'row'), 'col')  297 us
    another operation x6, other arithmetic, per_device(): panel_factor = jnp.linalg.cholesky(diagonal_block)  33.9 us
    dot_general x1, matrix products, per_device(): lax.dot_general(incoming[:, :, :strip_rows], incoming[:, :, strip_rows:],...  21.6 us
    another operation x4, other arithmetic, per_device(): jax.scipy.linalg.solve_triangular(panel_factor, tile_sum, lower=True)  21.1 us
    all_to_all x1, starting transfers between devices, per_device(): lax.all_to_all(outgoing, ('row', 'col'), split_axis=0, concat_axis=0, til...  12 us
    select_n x1, other arithmetic, per_device(): jnp.where(filled[:, None, None], jnp.concatenate([send_strip, send_tile],...  11.6 us
  transfers between devices with their start and end apart: 3, of which 2 were waited for; matrix products, arithmetic and copies ran while one was open for 14% of the time, Pallas kernels for 0%

profile of v2, /device:TPU:1, one launch (start us, length us, event | category | flops | bytes accessed | tf_op | source)
XLA Modules:
  0.0 446.0 jit_solution(14497599377031017640)
XLA Ops:
  7.2 0.7 broadcast_multiply_fusion.2
  7.8 0.8 copy.22
  8.6 0.1 copy.21
  8.7 0.1 mul.31
  8.8 0.1 eq.15
  8.9 0.1 fusion.17
  9.0 0.2 reduce_window_sum.11
  9.2 0.2 select_reduce_fusion
  9.4 1.0 scatter_custom_fusion
  10.4 0.8 fusion.18
  11.2 0.0 copy-start
  11.2 6.6 %gather_fusion.1 = f32[256,32,256]{2,1,0:T(8,128)} fusion(f32[128,32,256]{2,1,0:T(8,128)} %bitcast.43, s32[1024]{0:T(1024)S(1)} %get-tuple-element.34), kind=kCustom, calls=%fused_computation.1 | custom fusion | bytes 16778240 | tf_op jit(solution)/shard_map/gather | solution.py:35
  17.8 0.0 copy-done
  17.8 0.2 broadcast_multiply_fusion
  18.0 4.3 gather_fusion
  22.3 11.6 %maximum_select_fusion = f32[256,32,512]{2,1,0:T(8,128)} fusion(f32[256,32,256]{2,1,0:T(8,128)} %gather_fusion.1, f32[256,32,256]{2,1,0:T(8,128)} %gather_fusion, pred[256]{0:T(512)(128)(4,1)S(1)} %broadcast_compare_fusion), kind=kLoop, calls=%fused_computation.5 | loop fusion | flops 8388608 | bytes 33554688 | tf_op jit(solution)/shard_map/jit(_where)/select_n | solution.py:36
  34.0 12.0 %all-to-all-start = ((f32[256,32,512]{2,1,0:T(8,128)}), f32[256,32,512]{2,1,0:T(8,128)}, u32[]{:S(2)}, u32[]{:S(2)}) async-start(f32[256,32,512]{2,1,0:T(8,128)} %maximum_select_fusion), calls=%async_computation | async-start | bytes 33554432 | tf_op jit(solution)/shard_map/all_to_all | solution.py:39
  46.0 0.0 all-reduce.4.cloned.1.call-start
  46.0 2.7 convolution_bitcast_fusion
  48.7 0.0 all-reduce.4.cloned.1.call-update
  48.7 0.5 all-reduce.6.cloned.1.call-start
  49.2 165.3 %all-reduce.4.cloned.1.call-done = f32[256,256]{0,1:T(8,128)} async-done(((f32[256,256]{0,1:T(8,128)}), f32[256,256]{0,1:T(8,128)}) %all-reduce.4.cloned.1.call-update) | async-done | bytes 262160 | tf_op jit(solution)/shard_map/psum | solution.py:19
  214.6 0.0 all-reduce.6.cloned.1.call-update
  214.6 131.8 %all-reduce.6.cloned.1.call-done = f32[256,256]{0,1:T(8,128)} async-done(((f32[256,256]{0,1:T(8,128)}), f32[256,256]{0,1:T(8,128)}) %all-reduce.6.cloned.1.call-update) | async-done | bytes 262160 | tf_op jit(solution)/shard_map/psum | solution.py:19
  346.4 1.1 copy.20
  347.5 1.0 fusion.8
  348.5 11.7 %cholesky.51 = f32[128,128]{1,0:T(8,128)S(1)} custom-call(f32[128,128]{1,0:T(8,128)S(1)} %cholesky.121), custom_call_target="Cholesky" | custom-call | tf_op jit(solution)/shard_map/jit(cholesky)/cholesky | solution.py:46
  360.2 9.8 %custom-call.15 = f32[1,128,128]{1,2,0:T(8,128)S(1)} custom-call(f32[1,128,128]{2,1,0:T(8,128)S(1)} %get-tuple-element.27), custom_call_target="InvertDiagBlocksLowerTriangular" | custom-call | tf_op jit(solution)/shard_map/jit(cholesky)/cholesky | solution.py:46
  370.1 0.2 constant_dynamic-update-slice_fusion.1
  370.3 0.3 convolution_subtract_fusion.1
  370.5 11.7 %cholesky.107 = f32[128,128]{1,0:T(8,128)S(1)} custom-call(f32[128,128]{1,0:T(8,128)S(1)} %convolution_subtract_fusion.1), custom_call_target="Cholesky" | custom-call | tf_op jit(solution)/shard_map/jit(cholesky)/cholesky | solution.py:46
  382.3 0.6 compare_reduce_fusion
  384.2 0.7 fusion.9
  385.0 0.1 triangular_solve.44
  385.0 4.0 while.1
  385.1 0.6 fusion.30
  385.6 1.4 bitcast_dynamic-update-slice_fusion.2
  387.1 0.6 fusion.30
  387.7 1.4 bitcast_dynamic-update-slice_fusion.2
  389.1 19.7 %custom-call.16 = f32[2,128,128]{1,2,0:T(8,128)S(1)} custom-call(f32[2,128,128]{2,1,0:T(8,128)S(1)} %get-tuple-element.9), custom_call_target="InvertDiagBlocksLowerTriangular" | custom-call | tf_op jit(solution)/shard_map/jit(_solve_triangular)/triangular_solve | solution.py:47
  408.8 0.0 all-to-all-done
  408.8 6.9 %fusion.23 = (f32[256,32,256]{2,1,0:T(8,128)S(1)}, f32[256,32,256]{2,1,0:T(8,128)S(1)}) fusion(f32[256,32,512]{2,1,0:T(8,128)} %all-to-all-done), kind=kLoop, calls=%fused_computation.57 | loop fusion | bytes 33554432 | tf_op jit(solution)/shard_map/slice | solution.py:41
  415.7 21.6 %fusion.3 = f32[256,256]{1,0:T(8,128)S(1)} fusion(f32[256,32,256]{2,1,0:T(8,128)S(1)} %get-tuple-element.23, f32[256,32,256]{2,1,0:T(8,128)S(1)} %get-tuple-element.22), kind=kOutput, calls=%fused_computation.9 | convolution fusion | flops 6442450944 | bytes 17039360 | tf_op jit(solution)/shard_map/dot_general | solution.py:40
  437.3 0.3 fusion.10
  437.7 0.3 convolution_subtract_fusion
  437.9 0.3 fusion.13
  438.2 0.7 pad_maximum_fusion
  (13 shorter events, 0.1 us)
Async XLA Ops:
  11.2 6.6 %copy-start = (f32[32,32,256]{2,1,0:T(8,128)S(1)}, f32[32,32,256]{2,1,0:T(8,128)}, u32[]{:S(2)}) copy-start(f32[32,32,256]{2,1,0:T(8,128)} %param.5) | copy-start | bytes 3145732
  34.0 374.8 %all-to-all-start = ((f32[256,32,512]{2,1,0:T(8,128)}), f32[256,32,512]{2,1,0:T(8,128)}, u32[]{:S(2)}, u32[]{:S(2)}) async-start(f32[256,32,512]{2,1,0:T(8,128)} %maximum_select_fusion), calls=%async_computation | async-start | bytes 33554432 | tf_op jit(solution)/shard_map/all_to_all | solution.py:39
  46.0 168.6 %all-reduce.4.cloned.1.call-start = ((), (), s32[]{:S(2)}) async-start(), calls=%async_computation.1 | async-start | bytes 524288 | tf_op jit(solution)/shard_map/psum | solution.py:19
  48.7 297.7 %all-reduce.6.cloned.1.call-start = ((), (), s32[]{:S(2)}) async-start(), calls=%async_computation.2 | async-start | bytes 524288 | tf_op jit(solution)/shard_map/psum | solution.py:19
Sparse Core Ops, SparseCore 0:
  49.7 164.8 all-reduce.3
  218.1 128.2 all-reduce.5
